TPU v7x, 32 devices: a whole 2x2x4 slice. The times are simulated.
32 devices in a mesh: pole: 4 (over x, core), row: 4 (over z), col: 2 (over y).
Axes of the slice: x: 2, y: 2, z: 4, core: 2. Of those that a mesh axis runs over, the one named last changes fastest.
Arguments:
- green: bfloat16 [4, 4096, 4096], P('pole', 'row', 'col'), may hold values from -6 to 6
- factor: bfloat16 [4, 4096, 1024], P('pole', 'row', 'col'), may hold values from -0.09375 to 0.09375
- diag_inverse: bfloat16 [4, 512, 1024], P('pole', 'row', 'col'), may hold values from -6 to 6
- pole_weight: float32 [4], P('pole'), may hold values from 0.25 to 1
- pattern: int32 [8, 2], replicated, may hold values 0 or 1
Outputs:
- off_density: float32 [4096, 1024], P(('row', 'pole'), 'col')
- diag_density: float32 [512, 1024], P(('pole', 'row'), 'col')
All inputs are finite; a program needn't handle non-finite values.
Results may differ from a plain program's by a relative error of at most 0.005.
Values may be sent and summed in bfloat16 or wider, within the bound.
No kernel may reach another device: no remote copies, remote signals or barrier semaphores. Data moves between devices by JAX's collectives and lax.ppermute only.
A program may use at most 64 MiB of HBM per device.

v0:
```python
import jax
import jax.numpy as jnp
from jax import lax
from jax.sharding import PartitionSpec as P

BLOCK = 512
ANC = 8


def body(green, factor, diag_inverse, pole_weight, pattern):
    poles_here = green.shape[0]
    local_rows = factor.shape[1]
    local_cols = factor.shape[2]
    level_count = pattern.shape[1]
    row_at = lax.axis_index("row")
    col_at = lax.axis_index("col")
    row_ids = (row_at * local_rows + jnp.arange(local_rows, dtype=jnp.int32)) // BLOCK
    col_ids = (col_at * local_cols + jnp.arange(local_cols, dtype=jnp.int32)) // BLOCK
    row_onehot = (row_ids[:, None] == jnp.arange(ANC, dtype=jnp.int32)[None, :]).astype(jnp.float32)
    col_onehot = (col_ids[:, None] == jnp.arange(level_count, dtype=jnp.int32)[None, :]).astype(
        jnp.float32
    )
    pattern_f = pattern.astype(jnp.float32)
    keep_mask = jnp.dot(jnp.dot(row_onehot, pattern_f), col_onehot.T)
    masked = factor * keep_mask.astype(jnp.bfloat16)[None]
    whole_rows = lax.all_gather(green, "col", axis=2, tiled=True)
    product = jnp.einsum(
        "pij,pjk->pik",
        whole_rows,
        lax.all_gather(masked, "row", axis=1, tiled=True),
        preferred_element_type=jnp.float32,
    )
    update = (product * keep_mask[None]).astype(jnp.bfloat16)
    weights = pole_weight[:, None, None]
    off_term = -jnp.sum(weights * update.astype(jnp.float32), axis=0)
    level_here = local_cols // BLOCK
    factor_split = masked.reshape(poles_here, local_rows, level_here, BLOCK)
    update_split = update.reshape(poles_here, local_rows, level_here, BLOCK)
    cross_term = jnp.einsum(
        "prka,prkb->pakb", factor_split, update_split, preferred_element_type=jnp.float32
    )
    cross_term = cross_term.reshape(poles_here, BLOCK, local_cols)
    diag_term = -jnp.sum(weights * cross_term, axis=0)
    dinv_count = diag_inverse.shape[1]
    dinv_rows = jnp.sum(weights * diag_inverse.astype(jnp.float32), axis=0)
    current = lax.dynamic_slice_in_dim(diag_term, row_at * dinv_count, dinv_count, 0)
    diag_term = lax.dynamic_update_slice_in_dim(
        diag_term, current + dinv_rows, row_at * dinv_count, 0
    )
    off_density, pole_part = (
        lax.psum_scatter(off_term, "pole", scatter_dimension=0, tiled=True),
        lax.psum_scatter(diag_term, "pole", scatter_dimension=0, tiled=True),
    )
    diag_density = lax.psum_scatter(pole_part, "row", scatter_dimension=0, tiled=True)
    return (off_density, diag_density)


def solution(mesh):
    in_specs = (
        P("pole", "row", "col"),
        P("pole", "row", "col"),
        P("pole", "row", "col"),
        P("pole"),
        P(),
    )
    out_specs = (P(("row", "pole"), "col"), P(("pole", "row"), "col"))
    return jax.shard_map(body, mesh=mesh, in_specs=in_specs, out_specs=out_specs, check_vma=False)
```

profile of v0, /device:TPU:0, one launch (start us, length us, event | category | flops | bytes accessed | tf_op | source)
XLA Modules:
  0.0 296.8 jit_solution(12370110417123104437)
XLA Ops:
  7.2 0.0 all-gather.3.cloned.1.call-start
  7.3 2.9 bitcast_multiply_fusion.1
  10.1 0.0 all-gather.3.cloned.1.call-update
  10.2 0.0 copy-start.2
  10.2 0.0 all-gather.5.cloned.1.call-start
  10.2 0.7 all-gather.5.cloned.1.call-update
  10.9 0.0 reduce-scatter.8.cloned.1.call-start
  11.6 0.0 copy-done.2
  11.6 0.1 copy.11
  11.8 82.0 %all-gather.3.cloned.1.call-done = bf16[1,4096,512]{2,1,0:T(8,128)(2,1)} async-done(((bf16[1,1024,512]{2,1,0:T(8,128)(2,1)}), bf16[1,4096,512]{2,1,0:T(8,128)(2,1)}) %all-gather.3.cloned.1.call-update) | async-done | bytes 4194320 | tf_op jit(solution)/shard_map/all_gather | solution.py:30
  93.8 104.0 %all-gather.5.cloned.1.call-done = bf16[1,1024,4096]{2,1,0:T(8,128)(2,1)} async-done(((bf16[1,1024,2048]{2,1,0:T(8,128)(2,1)}), bf16[1,1024,4096]{2,1,0:T(8,128)(2,1)}) %all-gather.5.cloned.1.call-update) | async-done | bytes 8388624 | tf_op jit(solution)/shard_map/all_gather | solution.py:26
  197.8 0.0 copy-start
  197.8 10.5 %multiply_negate_fusion = (f32[1024,512]{1,0:T(8,128)}, bf16[1024,512]{1,0:T(8,128)(2,1)S(1)}) fusion(f32[]{:T(128)} %bitcast.41, f32[1024,512]{1,0:T(8,128)S(1)} %get-tuple-element.7, bf16[1,4096,512]{2,1,0:T(8,128)(2,1)} %all-gather.3.cloned.1.call-done, bf16[1,1024,4096]{2,1,0:T(8,128)(2,1)} %all-gather.5.cloned.1.call-done), kind=kOutput, calls=%fused_computation.5 | convolution fusion | flops 4297588736 | bytes 17825796 | tf_op jit(solution)/shard_map/pij,pjk->pik/dot_general | solution.py:27
  208.3 0.0 copy-done
  208.3 0.7 fusion.8
  209.0 0.1 copy.16
  209.2 0.0 copy-start.1
  209.2 1.0 copy-done.1
  210.2 0.0 reduce-scatter.8.cloned.1.call-update
  210.2 0.0 reduce-scatter.10.cloned.1.call-start
  210.2 24.9 %reduce-scatter.8.cloned.1.call-done = f32[128,512]{0,1:T(8,128)} async-done(((f32[512,512]{0,1:T(8,128)}), f32[128,512]{0,1:T(8,128)}) %reduce-scatter.8.cloned.1.call-update) | async-done | bytes 262160 | tf_op jit(solution)/shard_map/reduce_scatter | solution.py:52
  235.2 1.8 copy.14
  236.9 0.0 reduce-scatter.10.cloned.1.call-update
  237.0 0.0 reduce-scatter.6.cloned.1.call-start
  237.0 0.5 reduce-scatter.6.cloned.1.call-update
  237.6 20.3 %reduce-scatter.10.cloned.1.call-done = f32[32,512]{1,0:T(8,128)} async-done(((f32[128,512]{1,0:T(8,128)}), f32[32,512]{1,0:T(8,128)}) %reduce-scatter.10.cloned.1.call-update) | async-done | bytes 65552
  257.9 32.4 %reduce-scatter.6.cloned.1.call-done = f32[256,512]{1,0:T(8,128)} async-done(((f32[1024,512]{1,0:T(8,128)}), f32[256,512]{1,0:T(8,128)}) %reduce-scatter.6.cloned.1.call-update) | async-done | bytes 524304 | tf_op jit(solution)/shard_map/reduce_scatter | solution.py:51
  (3 shorter events, 0.1 us)
Async XLA Ops:
  7.2 86.6 %all-gather.3.cloned.1.call-start = ((), (), s32[]{:S(2)}) async-start(), calls=%async_computation.3 | async-start | bytes 5242880 | tf_op jit(solution)/shard_map/all_gather | solution.py:30
  10.2 1.5 copy-start.2
  10.2 187.7 %all-gather.5.cloned.1.call-start = ((), (), s32[]{:S(2)}) async-start(), calls=%async_computation.4 | async-start | bytes 12582912 | tf_op jit(solution)/shard_map/all_gather | solution.py:26
  10.9 224.2 %reduce-scatter.8.cloned.1.call-start = ((), (), s32[]{:S(2)}) async-start(), calls=%async_computation.6 | async-start | bytes 1310720 | tf_op jit(solution)/shard_map/reduce_scatter | solution.py:52
  197.8 10.5 %copy-start = (bf16[1,1024,512]{2,1,0:T(8,128)(2,1)S(1)}, bf16[1,1024,512]{2,1,0:T(8,128)(2,1)}, u32[]{:S(2)}) copy-start(bf16[1,1024,512]{2,1,0:T(8,128)(2,1)} %get-tuple-element.6) | copy-start | bytes 3145732
  209.2 1.0 copy-start.1
  210.2 47.7 %reduce-scatter.10.cloned.1.call-start = ((), (), s32[]{:S(2)}) async-start(), calls=%async_computation.7 | async-start | bytes 327680
  237.0 53.3 %reduce-scatter.6.cloned.1.call-start = ((), (), s32[]{:S(2)}) async-start(), calls=%async_computation.5 | async-start | bytes 2621440 | tf_op jit(solution)/shard_map/reduce_scatter | solution.py:51
Sparse Core Ops, SparseCore 0:
  10.3 83.4 all-gather.2
  95.3 102.4 all-gather.4
  210.3 24.8 reduce-scatter.7
  237.8 19.9 reduce-scatter.9
  260.8 29.4 reduce-scatter.5
where the time goes:
time: 297 us
  waiting for transfers between devices  265 us (89%)
  between operations  14.5 us (5%)
  matrix products  14.1 us (5%)
    all_gather x1, waiting for transfers between devices, body(): whole_rows = lax.all_gather(green, 'col', axis=2, tiled=True)  104 us
    all_gather x1, waiting for transfers between devices, body(): lax.all_gather(masked, 'row', axis=1, tiled=True)  82 us
    reduce_scatter x1, waiting for transfers between devices, body(): lax.psum_scatter(off_term, 'pole', scatter_dimension=0, tiled=True)  32.4 us
    reduce_scatter x1, waiting for transfers between devices, body(): lax.psum_scatter(diag_term, 'pole', scatter_dimension=0, tiled=True)  24.9 us
    unnamed x6, waiting for transfers between devices  21.6 us
    dot_general x1, matrix products, body(): jnp.einsum('pij,pjk->pik', whole_rows, lax.all_gather(masked, 'row', axis...  10.5 us
  transfers between devices with their start and end apart: 5, of which 5 were waited for; matrix products, arithmetic and copies ran while one was open for 0% of the time, Pallas kernels for 0%

commit v1 on v0

--- a/solution.py
+++ b/solution.py
@@ -24,12 +24,27 @@
     keep_mask = jnp.dot(jnp.dot(row_onehot, pattern_f), col_onehot.T)
     masked = factor * keep_mask.astype(jnp.bfloat16)[None]
     whole_rows = lax.all_gather(green, "col", axis=2, tiled=True)
-    product = jnp.einsum(
+    length, index = (lax.axis_size("row"), lax.axis_index("row"))
+    behind = [(i, (i - 1) % length) for i in range(length)]
+    width = masked.shape[1]
+    carried = masked
+    running = jnp.einsum(
         "pij,pjk->pik",
-        whole_rows,
-        lax.all_gather(masked, "row", axis=1, tiled=True),
+        lax.dynamic_slice_in_dim(whole_rows, index * width, carried.shape[1], axis=2),
+        carried,
         preferred_element_type=jnp.float32,
     )
+    for step in range(1, length):
+        carried = lax.ppermute(carried, "row", behind)
+        running = running + jnp.einsum(
+            "pij,pjk->pik",
+            lax.dynamic_slice_in_dim(
+                whole_rows, (index + step) % length * width, carried.shape[1], axis=2
+            ),
+            carried,
+            preferred_element_type=jnp.float32,
+        )
+    product = running
     update = (product * keep_mask[None]).astype(jnp.bfloat16)
     weights = pole_weight[:, None, None]
     off_term = -jnp.sum(weights * update.astype(jnp.float32), axis=0)

time: 297 us -> 216 us (0.73)
  waiting for transfers between devices: 265 us -> 171 us
  starting transfers between devices: 0.2 us -> 13.8 us
    all_gather x1 -> x0, waiting for transfers between devices: 82 us -> none  [body(): lax.all_gather(masked, 'row', axis=1, tiled=True)]
    all_gather x1, waiting for transfers between devices: 104 us -> 47.4 us  [body(): whole_rows = lax.all_gather(green, 'col', axis=2, tiled=True)]
    ppermute x0 -> x3, waiting for transfers between devices: none -> 44.3 us  [body(): carried = lax.ppermute(carried, 'row', behind)]
    ppermute x0 -> x3, starting transfers between devices: none -> 13.6 us  [body(): carried = lax.ppermute(carried, 'row', behind)]
    dot_general x1 -> x4, matrix products: 10.5 us -> 9.79 us  [the longest x3 8.55 us: body(): jnp.einsum('pij,pjk->pik', lax.dynamic_slice_in_dim(whole_rows, (index +...]
    unnamed x6 -> x5, waiting for transfers between devices: 21.6 us -> 21.7 us
  transfers between devices with their start and end apart: 5 -> 7, of which waited for: 5 -> 6; matrix products, arithmetic and copies ran while one was open for 0% -> 4% of each run, Pallas kernels for 0% -> 0%
where the time goes in v1:
time: 216 us
  waiting for transfers between devices  171 us (79%)
  between operations  14.6 us (7%)
  starting transfers between devices  13.8 us (6%)
  matrix products  12.2 us (6%)
  local copies, waits for them, and re-layouts  4.42 us (2%)
    all_gather x1, waiting for transfers between devices, body(): whole_rows = lax.all_gather(green, 'col', axis=2, tiled=True)  47.4 us
    ppermute x3, waiting for transfers between devices, body(): carried = lax.ppermute(carried, 'row', behind)  44.3 us
    reduce_scatter x1, waiting for transfers between devices, body(): lax.psum_scatter(off_term, 'pole', scatter_dimension=0, tiled=True)  32.4 us
    reduce_scatter x1, waiting for transfers between devices, body(): lax.psum_scatter(diag_term, 'pole', scatter_dimension=0, tiled=True)  24.9 us
    unnamed x5, waiting for transfers between devices  21.7 us
    ppermute x3, starting transfers between devices, body(): carried = lax.ppermute(carried, 'row', behind)  13.6 us
    dot_general x3, matrix products, body(): jnp.einsum('pij,pjk->pik', lax.dynamic_slice_in_dim(whole_rows, (index +...  8.55 us
    unnamed x19, local copies, waits for them, and re-layouts  4.42 us
  transfers between devices with their start and end apart: 7, of which 6 were waited for; matrix products, arithmetic and copies ran while one was open for 4% of the time, Pallas kernels for 0%

profile of v1, /device:TPU:0, one launch (start us, length us, event | category | flops | bytes accessed | tf_op | source)
XLA Modules:
  0.0 215.8 jit_solution(4423911990185290225)
XLA Ops:
  7.2 0.0 copy-start.1
  7.2 0.0 copy-start.5
  7.2 0.0 all-gather.2.cloned.1.call-start
  7.2 0.7 all-gather.2.cloned.1.call-update
  7.9 0.0 reduce-scatter.8.cloned.1.call-start
  8.0 0.4 copy-done.1
  8.4 0.0 copy-done.5
  8.4 0.0 copy-start.4
  8.4 1.7 bitcast_multiply_fusion
  10.1 5.1 %collective-permute-start = (bf16[1,1024,512]{2,1,0:T(8,128)(2,1)}, bf16[1,1024,512]{2,1,0:T(8,128)(2,1)S(1)}, u32[]{:S(2)}, u32[]{:S(2)}) collective-permute-start(bf16[1,1024,512]{2,1,0:T(8,128)(2,1)} %get-tuple-element.6), channel_id=1, source_target_pairs={{0,6},{2,0},{4,2},{6,4},{1,7},{3,1},{5,3},{7,5},{8,14},{10,8},{12,... | collective-permute-start | bytes 3145736 | tf_op jit(solution)/shard_map/ppermute | solution.py:38
  15.2 22.7 %collective-permute-done = bf16[1,1024,512]{2,1,0:T(8,128)(2,1)S(1)} collective-permute-done((bf16[1,1024,512]{2,1,0:T(8,128)(2,1)}, bf16[1,1024,512]{2,1,0:T(8,128)(2,1)S(1)}, u32[]{:S(2)}, u32[]{:S(2)}) %collective-permute-start) | collective-permute-done | bytes 1048608 | tf_op jit(solution)/shard_map/ppermute | solution.py:38
  37.9 0.0 copy-start.6
  37.9 4.2 %collective-permute-start.1 = (bf16[1,1024,512]{2,1,0:T(8,128)(2,1)S(1)}, bf16[1,1024,512]{2,1,0:T(8,128)(2,1)}, u32[]{:S(2)}, u32[]{:S(2)}) collective-permute-start(bf16[1,1024,512]{2,1,0:T(8,128)(2,1)S(1)} %collective-permute-done), channel_id=1, source_target_pairs={{0,6},{2,0},{4,2},{6,4},{1,7},{3,1},{5,3},{7,5},{8,14},{10,8},{12,... | collective-permute-start | bytes 3145736 | tf_op jit(solution)/shard_map/ppermute | solution.py:38
  42.1 21.6 %collective-permute-done.1 = bf16[1,1024,512]{2,1,0:T(8,128)(2,1)} collective-permute-done((bf16[1,1024,512]{2,1,0:T(8,128)(2,1)S(1)}, bf16[1,1024,512]{2,1,0:T(8,128)(2,1)}, u32[]{:S(2)}, u32[]{:S(2)}) %collective-permute-start.1) | collective-permute-done | bytes 1048608 | tf_op jit(solution)/shard_map/ppermute | solution.py:38
  63.6 4.4 %collective-permute-start.2 = (bf16[1,1024,512]{2,1,0:T(8,128)(2,1)}, bf16[1,1024,512]{2,1,0:T(8,128)(2,1)}, u32[]{:S(2)}, u32[]{:S(2)}) collective-permute-start(bf16[1,1024,512]{2,1,0:T(8,128)(2,1)} %collective-permute-done.1), channel_id=1, source_target_pairs={{0,6},{2,0},{4,2},{6,4},{1,7},{3,1},{5,3},{7,5},{8,14},{10,8},{12,... | collective-permute-start | bytes 3145736 | tf_op jit(solution)/shard_map/ppermute | solution.py:38
  68.0 0.0 copy-done.6
  68.7 0.0 copy-done.4
  68.7 0.1 copy.9
  68.8 0.0 copy-start.2
  68.8 47.4 %all-gather.2.cloned.1.call-done = bf16[1,1024,4096]{2,1,0:T(8,128)(2,1)} async-done(((bf16[1,1024,2048]{2,1,0:T(8,128)(2,1)}), bf16[1,1024,4096]{2,1,0:T(8,128)(2,1)}) %all-gather.2.cloned.1.call-update) | async-done | bytes 8388624 | tf_op jit(solution)/shard_map/all_gather | solution.py:26
  116.3 0.0 copy-start.3
  116.3 3.3 %fusion.2 = f32[1024,512]{1,0:T(8,128)S(1)} fusion(bf16[1,1024,4096]{2,1,0:T(8,128)(2,1)} %all-gather.2.cloned.1.call-done, s32[]{:T(128)S(6)} %select_n.55, bf16[1,1024,512]{2,1,0:T(8,128)(2,1)} %collective-permute-done.1), kind=kOutput, calls=%fused_computation.2 | convolution fusion | flops 1073741824 | bytes 5242884 | tf_op jit(solution)/shard_map/pij,pjk->pik/dot_general | solution.py:39
  119.5 0.0 copy-done.2
  119.5 1.1 copy-done.3
  120.6 0.0 copy-start.7
  120.6 1.2 fusion.6
  121.9 0.0 copy-done.7
  121.9 1.3 fusion.4
  123.1 0.0 collective-permute-done.2
  123.1 4.0 %multiply_negate_fusion = (f32[1024,512]{1,0:T(8,128)}, bf16[1024,512]{1,0:T(8,128)(2,1)S(1)}) fusion(f32[]{:T(128)} %bitcast.52, f32[1024,512]{1,0:T(8,128)S(1)} %get-tuple-element.7, bf16[1,1024,512]{2,1,0:T(8,128)(2,1)} %collective-permute-done.2, bf16[1,1024,4096]{2,1,0:T(8,128)(2,1)S(1)} %copy-done.3, s32[]{:T(128)S(6)} %select_n.57, ...), kind=kOutput, calls=%fused_computation.8 | convolution fusion | flops 1077936128 | bytes 14680072 | tf_op jit(solution)/shard_map/pij,pjk->pik/dot_general | solution.py:39
  127.2 0.7 fusion.14
  127.9 0.1 copy.13
  128.1 0.0 copy-start
  128.1 1.0 copy-done
  129.0 0.0 reduce-scatter.8.cloned.1.call-update
  129.0 0.0 reduce-scatter.10.cloned.1.call-start
  129.1 24.9 %reduce-scatter.8.cloned.1.call-done = f32[128,512]{0,1:T(8,128)} async-done(((f32[512,512]{0,1:T(8,128)}), f32[128,512]{0,1:T(8,128)}) %reduce-scatter.8.cloned.1.call-update) | async-done | bytes 262160 | tf_op jit(solution)/shard_map/reduce_scatter | solution.py:67
  154.0 1.8 copy.11
  155.8 0.0 reduce-scatter.10.cloned.1.call-update
  155.8 0.0 reduce-scatter.6.cloned.1.call-start
  155.9 0.5 reduce-scatter.6.cloned.1.call-update
  156.4 20.5 %reduce-scatter.10.cloned.1.call-done = f32[32,512]{1,0:T(8,128)} async-done(((f32[128,512]{1,0:T(8,128)}), f32[32,512]{1,0:T(8,128)}) %reduce-scatter.10.cloned.1.call-update) | async-done | bytes 65552
  176.8 32.4 %reduce-scatter.6.cloned.1.call-done = f32[256,512]{1,0:T(8,128)} async-done(((f32[1024,512]{1,0:T(8,128)}), f32[256,512]{1,0:T(8,128)}) %reduce-scatter.6.cloned.1.call-update) | async-done | bytes 524304 | tf_op jit(solution)/shard_map/reduce_scatter | solution.py:66
  (3 shorter events, 0.1 us)
Async XLA Ops:
  7.2 1.2 copy-start.1
  7.2 1.2 copy-start.5
  7.2 109.1 %all-gather.2.cloned.1.call-start = ((), (), s32[]{:S(2)}) async-start(), calls=%async_computation.3 | async-start | bytes 12582912 | tf_op jit(solution)/shard_map/all_gather | solution.py:26
  7.9 146.1 %reduce-scatter.8.cloned.1.call-start = ((), (), s32[]{:S(2)}) async-start(), calls=%async_computation.5 | async-start | bytes 1310720 | tf_op jit(solution)/shard_map/reduce_scatter | solution.py:67
  8.4 60.3 %copy-start.4 = (bf16[1,128,512]{2,1,0:T(8,128)(2,1)S(1)}, bf16[1,128,512]{2,1,0:T(8,128)(2,1)}, u32[]{:S(2)}) copy-start(bf16[1,128,512]{2,1,0:T(8,128)(2,1)} %param.7) | copy-start | bytes 393220
  10.1 27.8 %collective-permute-start = (bf16[1,1024,512]{2,1,0:T(8,128)(2,1)}, bf16[1,1024,512]{2,1,0:T(8,128)(2,1)S(1)}, u32[]{:S(2)}, u32[]{:S(2)}) collective-permute-start(bf16[1,1024,512]{2,1,0:T(8,128)(2,1)} %get-tuple-element.6), channel_id=1, source_target_pairs={{0,6},{2,0},{4,2},{6,4},{1,7},{3,1},{5,3},{7,5},{8,14},{10,8},{12,... | collective-permute-start | bytes 3145736 | tf_op jit(solution)/shard_map/ppermute | solution.py:38
  37.9 30.1 %copy-start.6 = (bf16[1,1024,512]{2,1,0:T(8,128)(2,1)}, bf16[1,1024,512]{2,1,0:T(8,128)(2,1)S(1)}, u32[]{:S(2)}) copy-start(bf16[1,1024,512]{2,1,0:T(8,128)(2,1)S(1)} %collective-permute-done) | copy-start | bytes 3145732
  37.9 25.7 %collective-permute-start.1 = (bf16[1,1024,512]{2,1,0:T(8,128)(2,1)S(1)}, bf16[1,1024,512]{2,1,0:T(8,128)(2,1)}, u32[]{:S(2)}, u32[]{:S(2)}) collective-permute-start(bf16[1,1024,512]{2,1,0:T(8,128)(2,1)S(1)} %collective-permute-done), channel_id=1, source_target_pairs={{0,6},{2,0},{4,2},{6,4},{1,7},{3,1},{5,3},{7,5},{8,14},{10,8},{12,... | collective-permute-start | bytes 3145736 | tf_op jit(solution)/shard_map/ppermute | solution.py:38
  63.6 59.5 %collective-permute-start.2 = (bf16[1,1024,512]{2,1,0:T(8,128)(2,1)}, bf16[1,1024,512]{2,1,0:T(8,128)(2,1)}, u32[]{:S(2)}, u32[]{:S(2)}) collective-permute-start(bf16[1,1024,512]{2,1,0:T(8,128)(2,1)} %collective-permute-done.1), channel_id=1, source_target_pairs={{0,6},{2,0},{4,2},{6,4},{1,7},{3,1},{5,3},{7,5},{8,14},{10,8},{12,... | collective-permute-start | bytes 3145736 | tf_op jit(solution)/shard_map/ppermute | solution.py:38
  68.8 50.7 %copy-start.2 = (bf16[1,1024,512]{2,1,0:T(8,128)(2,1)S(1)}, bf16[1,1024,512]{2,1,0:T(8,128)(2,1)}, u32[]{:S(2)}) copy-start(bf16[1,1024,512]{2,1,0:T(8,128)(2,1)} %get-tuple-element.6) | copy-start | bytes 3145732
  116.3 4.3 %copy-start.3 = (bf16[1,1024,4096]{2,1,0:T(8,128)(2,1)S(1)}, bf16[1,1024,4096]{2,1,0:T(8,128)(2,1)}, u32[]{:S(2)}) copy-start(bf16[1,1024,4096]{2,1,0:T(8,128)(2,1)} %all-gather.2.cloned.1.call-done) | copy-start | bytes 25165828
  120.6 1.2 copy-start.7
  128.1 1.0 copy-start
  129.0 47.8 %reduce-scatter.10.cloned.1.call-start = ((), (), s32[]{:S(2)}) async-start(), calls=%async_computation.6 | async-start | bytes 327680
  155.8 53.4 %reduce-scatter.6.cloned.1.call-start = ((), (), s32[]{:S(2)}) async-start(), calls=%async_computation.4 | async-start | bytes 2621440 | tf_op jit(solution)/shard_map/reduce_scatter | solution.py:66
Sparse Core Ops, SparseCore 0:
  9.5 106.6 all-gather.1
  129.2 24.7 reduce-scatter.7
  156.8 19.9 reduce-scatter.9
  179.8 29.4 reduce-scatter.5
